TPU v7x, 32 devices: a whole 2x2x4 slice. The times are simulated.
32 devices in a mesh: lat: 8 (over y, x, core), chan: 4 (over z).
Axes of the slice: x: 2, y: 2, z: 4, core: 2. Of those that a mesh axis runs over, the one named last changes fastest.
Arguments:
- state: bfloat16 [256, 64, 1440], P('chan', 'lat'), may hold values from -6 to 6
- kernel: bfloat16 [3, 3, 256, 256], replicated, may hold values from -0.125 to 0.125
- bias: float32 [256], P('chan'), may hold values from -3 to 3
- innovations: float32 [256, 8, 8, 1024], P('chan', 'lat'), may hold values from -6 to 6
- interp: bfloat16 [4, 8, 8, 1024], P(None, 'lat'), may hold values from 0 to 1
- cells: int32 [8, 8, 1024], P('lat'), may hold values from 0 to 90719, as said below
- counts: int32 [8, 8], P('lat'), may hold values from 1 to 1024, as said below
Outputs:
- grad_state: bfloat16 [256, 64, 1440], P('chan', 'lat')
- departures: float32 [256, 8, 8, 1024], P('chan', 'lat')
Inputs may be any that keep to these rules, and one draw needn't show every extreme that they name: `cells`: every observation of slab d has its first corner in rows 8 d to 8 d + 6. `counts`: in every draw some slab receives 1024 used slots from every instrument shard.
All inputs are finite; a program needn't handle non-finite values.
Results may differ from a plain program's by a relative error of at most 0.023.
Values may be sent and summed in bfloat16 or wider, within the bound.
No kernel may reach another device: no remote copies, remote signals or barrier semaphores. Data moves between devices by JAX's collectives and lax.ppermute only.
A program may use at most 256 MiB of HBM per device.

v0:
```python
import jax
import jax.numpy as jnp
from jax import lax
from jax.sharding import PartitionSpec as P

KERNEL_SPACING = 8


def extended(block, sides, width):
    for axis, dim in sides:
        count = lax.axis_size(axis)
        forward = [(i, i + 1) for i in range(count - 1)]
        backward = [(target, source) for source, target in forward]
        low = lax.ppermute(
            lax.slice_in_dim(block, block.shape[dim] - width, None, axis=dim), axis, forward
        )
        high = lax.ppermute(lax.slice_in_dim(block, 0, width, axis=dim), axis, backward)
        block = jnp.concatenate([low, block, high], axis=dim)
    return block


def gelu_value(value):
    return 0.5 * value * (1.0 + jax.scipy.special.erf(value * 0.7071067811865476))


def gelu_slope(value):
    return (
        0.5 * (1.0 + jax.scipy.special.erf(value * 0.7071067811865476))
        + value * jnp.exp(-0.5 * value * value) * 0.3989422804014327
    )


def tap_stack(padded_field, direction_sign, row_count):
    field_pieces = []
    for row_offset in range(3):
        for column_offset in range(3):
            start_offset = KERNEL_SPACING + direction_sign * (row_offset - 1) * KERNEL_SPACING
            part = lax.slice_in_dim(padded_field, start_offset, start_offset + row_count, axis=1)
            field_pieces.append(
                jnp.roll(part, -direction_sign * (column_offset - 1) * KERNEL_SPACING, axis=2)
            )
    stacked = jnp.stack(field_pieces)
    return stacked.reshape(9 * padded_field.shape[0], row_count * padded_field.shape[2])


def channel_mix(grid_field, kernel_t, direction_sign):
    group, row_count, width = grid_field.shape
    total_channels = kernel_t.shape[0]
    owner = lax.axis_index("chan")
    padded_field = extended(grid_field, (("lat", 1),), KERNEL_SPACING)
    stacked = tap_stack(padded_field, direction_sign, row_count)
    local_weights = lax.dynamic_slice_in_dim(kernel_t, owner * group, group, 3).reshape(
        total_channels, 9 * group
    )
    return lax.psum_scatter(
        jnp.dot(local_weights, stacked, preferred_element_type=jnp.float32)
        .reshape(group * lax.axis_size("chan"), row_count, width)
        .astype(jnp.bfloat16),
        "chan",
        scatter_dimension=0,
        tiled=True,
    ).astype(jnp.float32)


def shards(state, kernel, bias, innovations, interp, cells, counts):
    group, row_count, width = state.shape
    forward_kernel = jnp.transpose(kernel, (2, 0, 1, 3))
    backward_kernel = jnp.transpose(kernel, (3, 0, 1, 2))
    pre = channel_mix(state, forward_kernel, 1) + bias[:, None, None]
    hidden = gelu_value(pre)
    flat_hidden = hidden.reshape(group, row_count * width)
    slots = jnp.arange(innovations.shape[3], dtype=jnp.int32)
    mask = (slots[None, :] < counts[0][:, None]).astype(jnp.float32)
    masked_values = innovations * mask[None, None]
    masked_weights = interp.astype(jnp.float32) * mask[None, None]
    got_values, got_weights = (
        lax.all_to_all(
            masked_values.astype(jnp.bfloat16), "lat", split_axis=2, concat_axis=1, tiled=True
        ).astype(masked_values.dtype),
        lax.all_to_all(
            masked_weights.astype(jnp.bfloat16), "lat", split_axis=2, concat_axis=1, tiled=True
        ).astype(masked_weights.dtype),
    )
    got_cells = lax.all_to_all(cells, "lat", split_axis=1, concat_axis=0, tiled=True)
    local_cells = got_cells - lax.axis_index("lat") * row_count * width
    row_index = local_cells // width
    col_index = local_cells % width
    corner_one = row_index * width + (col_index + 1) % width
    corners = [local_cells, corner_one, local_cells + width, corner_one + width]
    model = jnp.zeros(got_values.shape, jnp.float32)
    for which in range(4):
        model = model + got_weights[which][None] * jnp.take(flat_hidden, corners[which], axis=1)
    local_departures = model - got_values
    departures = lax.all_to_all(
        local_departures.astype(jnp.bfloat16), "lat", split_axis=1, concat_axis=2, tiled=True
    ).astype(local_departures.dtype)
    grad_hidden = jnp.zeros((group, row_count * width), jnp.float32)
    for which in range(4):
        grad_hidden = grad_hidden.at[:, corners[which].reshape(-1)].add(
            (got_weights[which][None] * local_departures).reshape(group, -1)
        )
    grad_pre = (grad_hidden.reshape(pre.shape) * gelu_slope(pre)).astype(jnp.bfloat16)
    grad_state = channel_mix(grad_pre, backward_kernel, -1).astype(jnp.bfloat16)
    return (grad_state, departures)


def solution(mesh):
    return jax.shard_map(
        shards,
        mesh=mesh,
        in_specs=(
            P("chan", "lat", None),
            P(),
            P("chan"),
            P("chan", "lat", None, None),
            P(None, "lat", None, None),
            P("lat", None, None),
            P("lat", None),
        ),
        out_specs=(P("chan", "lat", None), P("chan", "lat", None, None)),
        check_vma=False,
    )
```

profile of v0, /device:TPU:0, one launch (start us, length us, event | category | flops | bytes accessed | tf_op | source)
XLA Modules:
  0.0 894.1 jit_solution(1340920264573949839)
XLA Ops:
  7.2 3.6 collective-permute-start
  10.9 1.3 collective-permute-start.1
  14.4 1.1 fusion.56
  15.5 2.9 fusion.58
  19.5 1.8 fusion.26
  21.4 2.7 bitcast_dynamic-update-slice_fusion.5
  24.0 1.3 fusion.27
  25.3 1.9 fusion.28
  27.3 1.2 bitcast_dynamic-update-slice_fusion.4
  28.5 1.4 fusion.29
  29.9 2.9 fusion.54
  32.9 1.1 fusion.55
  34.0 1.9 fusion.30
  35.8 2.7 bitcast_dynamic-update-slice_fusion.3
  38.5 1.3 fusion.31
  39.9 27.0 %reshape.416 = bf16[576,11520]{1,0:T(8,128)(2,1)} reshape(bf16[9,64,8,1440]{3,2,1,0:T(8,128)(2,1)} %fusion.31) | data formatting | bytes 26542080 | tf_op jit(solution)/shard_map/reshape | solution.py:43
  66.9 28.0 %dot_general.15 = bf16[8,1440,576]{1,0,2:T(8,128)(2,1)} reshape(bf16[11520,576]{0,1:T(8,128)(2,1)} %bitcast.220) | data formatting | bytes 26542080 | tf_op jit(solution)/shard_map/dot_general | solution.py:56
  94.8 24.5 %fusion.4 = bf16[256,8,1440]{2,0,1:T(8,128)(2,1)} fusion(bf16[256,576,1]{0,1,2:T(8,128)(2,1)S(1)} %bitcast.234, bf16[8,1440,576]{1,0,2:T(8,128)(2,1)} %dot_general.15), kind=kOutput, calls=%fused_computation.12 | convolution fusion | flops 3400335360 | bytes 19464192 | tf_op jit(solution)/shard_map/dot_general | solution.py:56
  120.7 33.1 %all-to-all-start = ((s32[1,8,1024]{2,0,1:T(1,128)}), s32[1,8,1024]{2,0,1:T(1,128)S(1)}, u32[]{:S(2)}, u32[]{:S(2)}) async-start(s32[1,8,1024]{2,0,1:T(1,128)} %copy.92), calls=%async_computation | async-start | bytes 65536 | tf_op jit(solution)/shard_map/all_to_all | solution.py:84
  153.9 2.1 fusion.25
  156.7 1.9 all-to-all-done
  158.6 3.4 all-to-all-start.1
  164.1 1.1 compare_select_fusion.5
  167.0 4.3 all-to-all-start.2
  171.3 89.6 %reduce-scatter.3.cloned.1.call-done = bf16[64,8,1440]{2,0,1:T(8,128)(2,1)} async-done(((bf16[256,8,1440]{2,0,1:T(8,128)(2,1)}), bf16[64,8,1440]{2,0,1:T(8,128)(2,1)}) %reduce-scatter.3.cloned.1.call-update) | async-done | bytes 1474576 | tf_op jit(solution)/shard_map/reduce_scatter | solution.py:55
  260.9 3.7 multiply_multiply_fusion.1
  264.6 5.7 copy.124
  270.2 30.6 %gather_fusion.2 = f32[8192,64]{1,0:T(8,128)} fusion(f32[64,11520]{0,1:T(8,128)} %bitcast.215, s32[8192]{0:T(1024)S(1)} %get-tuple-element.69), kind=kCustom, calls=%fused_computation.2.clone | custom fusion | bytes 4227072 | tf_op jit(solution)/shard_map/jit(_take)/gather | solution.py:92
  300.8 2.8 copy.103
  303.6 33.3 %gather_fusion.3 = f32[8192,64]{1,0:T(8,128)} fusion(f32[64,11520]{0,1:T(8,128)} %bitcast.216, s32[8192]{0:T(1024)} %get-tuple-element.68), kind=kCustom, calls=%fused_computation.3.clone | custom fusion | bytes 4227072 | tf_op jit(solution)/shard_map/jit(_take)/gather | solution.py:92
  336.9 3.8 copy.105
  340.7 33.3 %gather_fusion.1 = f32[8192,64]{1,0:T(8,128)} fusion(f32[64,11520]{0,1:T(8,128)} %bitcast.217, s32[8192]{0:T(1024)} %get-tuple-element.70), kind=kCustom, calls=%fused_computation.1.clone | custom fusion | bytes 4227072 | tf_op jit(solution)/shard_map/jit(_take)/gather | solution.py:92
  373.9 3.8 copy.101
  377.7 30.6 %gather_fusion = f32[8192,64]{1,0:T(8,128)} fusion(f32[64,11520]{0,1:T(8,128)} %bitcast.218, s32[8192]{0:T(1024)S(1)} %get-tuple-element.71), kind=kCustom, calls=%fused_computation.clone | custom fusion | bytes 4227072 | tf_op jit(solution)/shard_map/jit(_take)/gather | solution.py:92
  408.3 3.8 copy.99
  412.1 5.7 convert_bitcast_fusion
  417.8 2.9 broadcast_multiply_fusion
  420.9 2.7 copy.108
  423.6 1.7 copy.131
  425.4 2.8 copy.110
  428.2 1.7 copy.132
  429.9 2.8 copy.112
  432.7 1.7 copy.133
  434.5 2.8 copy.114
  437.3 47.2 %scatter_custom_fusion = f32[64,11520]{0,1:T(8,128)} fusion(s32[8192]{0:T(1024)} %bitcast.244, f32[8192,64]{1,0:T(8,128)} %copy.108, f32[]{:T(128)} %constant.32.clone.1), kind=kCustom, calls=%fused_computation.24 | custom fusion | flops 524288 | bytes 2949632 | tf_op jit(solution)/shard_map/scatter-add | solution.py:99
  484.4 45.1 %scatter_fusion = f32[64,11520]{0,1:T(8,128)} fusion(f32[64,11520]{0,1:T(8,128)} %scatter_custom_fusion, s32[8192]{0:T(1024)S(1)} %bitcast.239, f32[8192,64]{1,0:T(8,128)} %copy.110), kind=kCustom, calls=%fused_computation.5 | custom fusion | flops 524288 | bytes 6324224 | tf_op jit(solution)/shard_map/scatter-add | solution.py:99
  529.5 45.2 %scatter_fusion.1 = f32[64,11520]{0,1:T(8,128)} fusion(f32[64,11520]{0,1:T(8,128)} %scatter_fusion, s32[8192]{0:T(1024)S(1)} %bitcast.238, f32[8192,64]{1,0:T(8,128)} %copy.112), kind=kCustom, calls=%fused_computation.6 | custom fusion | flops 524288 | bytes 6324224 | tf_op jit(solution)/shard_map/scatter-add | solution.py:99
  574.7 45.1 %scatter_fusion.2 = f32[64,11520]{0,1:T(8,128)} fusion(f32[64,11520]{0,1:T(8,128)} %scatter_fusion.1, s32[8192]{0:T(1024)S(1)} %bitcast.237, f32[8192,64]{1,0:T(8,128)} %copy.114), kind=kCustom, calls=%fused_computation.7 | custom fusion | flops 524288 | bytes 6324224 | tf_op jit(solution)/shard_map/scatter-add | solution.py:99
  619.8 6.1 copy.116
  625.9 3.1 fusion.15
  629.0 1.3 collective-permute-start.2
  630.3 3.1 collective-permute-start.3
  633.6 1.2 fusion.51
  634.8 1.2 fusion.53
  638.2 1.2 fusion.49
  640.6 21.6 %copy.117 = bf16[9,64,8,1440]{3,2,1,0:T(8,128)(2,1)} copy(bf16[9,64,8,1440]{3,1,2,0:T(8,128)(2,1)S(1)} %fusion.37) | data formatting | bytes 26542080 | tf_op jit(solution)/shard_map/stack | solution.py:42
  662.3 26.8 %reshape.423 = bf16[576,11520]{1,0:T(8,128)(2,1)} reshape(bf16[9,64,8,1440]{3,2,1,0:T(8,128)(2,1)} %copy.117) | data formatting | bytes 26542080 | tf_op jit(solution)/shard_map/reshape | solution.py:43
  689.1 27.9 %dot_general.18 = bf16[8,1440,576]{1,0,2:T(8,128)(2,1)} reshape(bf16[11520,576]{0,1:T(8,128)(2,1)} %bitcast.221) | data formatting | bytes 26542080 | tf_op jit(solution)/shard_map/dot_general | solution.py:56
  717.0 24.7 %fusion.7 = bf16[256,8,1440]{2,0,1:T(8,128)(2,1)} fusion(bf16[256,576,1]{0,1,2:T(8,128)(2,1)S(1)} %bitcast.235, bf16[8,1440,576]{1,0,2:T(8,128)(2,1)} %dot_general.18), kind=kOutput, calls=%fused_computation.13 | convolution fusion | flops 3400335360 | bytes 19464192 | tf_op jit(solution)/shard_map/dot_general | solution.py:56
  741.7 1.2 copy-done.3
  742.9 49.0 %all_to_all.16 = bf16[64,8,1,1024]{3,0,2,1:T(8,128)(2,1)S(1)} all-to-all(bf16[64,8,1,1024]{3,0,2,1:T(8,128)(2,1)S(1)} %copy-done.3), channel_id=1, replica_groups=mesh['lat'=8,'chan'=4] {'lat'}, dimensions={1} | all-to-all | bytes 2097152 | tf_op jit(solution)/shard_map/all_to_all | solution.py:94
  792.2 2.5 copy.121
  794.7 88.7 %reduce-scatter.5.cloned.1.call-done = bf16[64,8,1440]{2,0,1:T(8,128)(2,1)} async-done(((bf16[256,8,1440]{2,0,1:T(8,128)(2,1)}), bf16[64,8,1440]{2,0,1:T(8,128)(2,1)}) %reduce-scatter.5.cloned.1.call-update) | async-done | bytes 1474576 | tf_op jit(solution)/shard_map/reduce_scatter | solution.py:55
  883.4 3.4 copy.120
  (67 shorter events, 13.3 us)
Async XLA Ops:
  7.2 5.0 copy-start
  7.2 7.3 copy-start.1
  7.2 253.7 %reduce-scatter.3.cloned.1.call-start = ((), (), s32[]{:S(2)}) async-start(), calls=%async_computation.6 | async-start | bytes 7864320 | tf_op jit(solution)/shard_map/reduce_scatter | solution.py:55
  7.2 8.3 collective-permute-start
  10.9 19.1 %collective-permute-start.1 = (bf16[64,8,1440]{2,1,0:T(8,128)(2,1)}, bf16[64,8,1440]{2,1,0:T(8,128)(2,1)}, u32[]{:S(2)}, u32[]{:S(2)}) collective-permute-start(bf16[64,8,1440]{2,1,0:T(8,128)(2,1)} %param.9), channel_id=1, source_target_pairs={{4,0},{8,4},{12,8},{16,12},{20,16},{24,20},{28,24},{5,1},{9,5},{13... | collective-permute-start | bytes 4423688 | tf_op jit(solution)/shard_map/ppermute | solution.py:17
  66.9 28.0 %copy-start.5 = (bf16[256,3,3,64]{0,3,2,1:T(8,128)(2,1)S(1)}, bf16[256,3,3,64]{0,3,2,1:T(8,128)(2,1)}, u32[]{:S(2)}) copy-start(bf16[256,3,3,64]{0,3,2,1:T(8,128)(2,1)} %copy.95) | copy-start | bytes 884740
  119.3 0.8 copy-start.9
  119.3 34.5 %copy-start.12 = (s32[1,8]{1,0:T(1,128)S(1)}, s32[1,8]{1,0:T(1,128)}, u32[]{:S(2)}) copy-start(s32[1,8]{1,0:T(1,128)} %param.15) | copy-start | bytes 100
  119.3 34.5 %copy-start.4 = (f32[64,1,8,1024]{3,2,1,0:T(8,128)S(1)}, f32[64,1,8,1024]{3,2,1,0:T(8,128)}, u32[]{:S(2)}) copy-start(f32[64,1,8,1024]{3,2,1,0:T(8,128)} %param.12) | copy-start | bytes 6291460
  120.1 35.9 %copy-start.6 = (bf16[4,1,8,1024]{3,2,1,0:T(8,128)(2,1)S(1)}, bf16[4,1,8,1024]{3,2,1,0:T(8,128)(2,1)}, u32[]{:S(2)}) copy-start(bf16[4,1,8,1024]{3,2,1,0:T(8,128)(2,1)} %param.13) | copy-start | bytes 196612
  120.7 37.9 %all-to-all-start = ((s32[1,8,1024]{2,0,1:T(1,128)}), s32[1,8,1024]{2,0,1:T(1,128)S(1)}, u32[]{:S(2)}, u32[]{:S(2)}) async-start(s32[1,8,1024]{2,0,1:T(1,128)} %copy.92), calls=%async_computation | async-start | bytes 65536 | tf_op jit(solution)/shard_map/all_to_all | solution.py:84
  156.0 104.8 %copy-start.10 = (f32[64]{0:T(128)S(1)}, f32[64]{0:T(128)}, u32[]{:S(2)}) copy-start(f32[64]{0:T(128)} %param.11) | copy-start | bytes 772
  158.6 8.3 all-to-all-start.1
  167.0 245.2 %all-to-all-start.2 = ((bf16[64,1,8,1024]{3,0,1,2:T(8,128)(2,1)}), bf16[64,1,8,1024]{3,0,1,2:T(8,128)(2,1)}, u32[]{:S(2)}, u32[]{:S(2)}) async-start(bf16[64,1,8,1024]{3,0,1,2:T(8,128)(2,1)} %fusion.25), calls=%async_computation.3 | async-start | bytes 2097152 | tf_op jit(solution)/shard_map/all_to_all | solution.py:77
  171.2 712.2 %reduce-scatter.5.cloned.1.call-start = ((), (), s32[]{:S(2)}) async-start(), calls=%async_computation.7 | async-start | bytes 7864320 | tf_op jit(solution)/shard_map/reduce_scatter | solution.py:55
  408.3 3.8 copy-start.7
  408.3 3.8 copy-start.8
  619.8 6.1 copy-start.2
  619.8 6.1 copy-start.11
  629.0 5.8 collective-permute-start.2
  630.3 7.9 collective-permute-start.3
  741.7 1.2 copy-start.3
Sparse Core Ops, SparseCore 0:
  119.5 141.3 reduce-scatter.2
  741.8 141.5 reduce-scatter.4
where the time goes:
time: 904 us; the launch traced here: 894 us
  local copies, waits for them, and re-layouts  333 us (37%)
  other arithmetic  217 us (24%)
  waiting for transfers between devices  181 us (20%)
  starting transfers between devices  50.1 us (6%)
  matrix products  49.2 us (5%)
  blocking collectives  49 us (5%)
  between operations  14.8 us (2%)
    scatter-add x4, other arithmetic, shards(): grad_hidden.at[:, corners[which].reshape(-1)]  183 us
    reduce_scatter x2, waiting for transfers between devices, channel_mix(): lax.psum_scatter(jnp.dot(local_weights, stacked, preferred_element_type=j...  178 us
    gather x8, local copies, waits for them, and re-layouts, shards(): jnp.take(flat_hidden, corners[which], axis=1)  142 us
    dot_general x2, local copies, waits for them, and re-layouts, channel_mix(): jnp.dot(local_weights, stacked, preferred_element_type=jnp.float32)  55.9 us
    reshape x2, local copies, waits for them, and re-layouts, tap_stack(): stacked.reshape(9 * padded_field.shape[0], row_count * padded_field.shape...  53.8 us
    dot_general x2, matrix products, channel_mix(): jnp.dot(local_weights, stacked, preferred_element_type=jnp.float32)  49.2 us
    all_to_all x1, blocking collectives, shards(): lax.all_to_all(local_departures.astype(jnp.bfloat16), 'lat', split_axis=1...  49 us
    all_to_all x1, starting transfers between devices, shards(): lax.all_to_all(cells, 'lat', split_axis=1, concat_axis=0, tiled=True)  33.1 us
  transfers between devices with their start and end apart: 9, of which 4 were waited for; matrix products, arithmetic and copies ran while one was open for 21% of the time, Pallas kernels for 0%

commit v1 on v0

--- a/solution.py
+++ b/solution.py
@@ -4,6 +4,34 @@
 from jax.sharding import PartitionSpec as P
 
 KERNEL_SPACING = 8
+
+
+def change_rings(packet, dim_k, message):
+    reply, found_now = (packet.shape[:dim_k], packet.shape[dim_k + 1 :])
+    return jnp.moveaxis(packet.reshape(*reply, message, -1, *found_now), dim_k, 0)
+
+
+def attach_keys_on_mesh(field_in, array_axis):
+    field_in = jnp.moveaxis(field_in, 0, array_axis)
+    piece_next = field_in.shape
+    return field_in.reshape(
+        *piece_next[:array_axis],
+        piece_next[array_axis] * piece_next[array_axis + 1],
+        *piece_next[array_axis + 2 :]
+    )
+
+
+def panel_set(sheet, axis_key, vector, my_data):
+    x_next, carry_out = (lax.axis_size(axis_key), lax.axis_index(axis_key))
+    everything = change_rings(sheet, vector, x_next)
+    blocks_here = [everything[carry_out]]
+    for pp in range(1, x_next):
+        current_arr = everything[carry_out ^ pp]
+        blocks_here.append(
+            lax.ppermute(current_arr, axis_key, [(q, q ^ pp) for q in range(x_next)])
+        )
+    everything = jnp.stack(blocks_here)[carry_out ^ jnp.arange(x_next)]
+    return attach_keys_on_mesh(everything, my_data)
 
 
 def extended(block, sides, width):
@@ -81,7 +109,7 @@
             masked_weights.astype(jnp.bfloat16), "lat", split_axis=2, concat_axis=1, tiled=True
         ).astype(masked_weights.dtype),
     )
-    got_cells = lax.all_to_all(cells, "lat", split_axis=1, concat_axis=0, tiled=True)
+    got_cells = panel_set(cells, "lat", 1, 0)
     local_cells = got_cells - lax.axis_index("lat") * row_count * width
     row_index = local_cells // width
     col_index = local_cells % width

time: 904 us -> 904 us (level)
    ppermute x0 -> x7, starting transfers between devices: none -> 37.1 us  [panel_set(): lax.ppermute(current_arr, axis_key, [(q, q ^ pp) for q in range(x_next)])]
    all_to_all x1 -> x0, starting transfers between devices: 33.1 us -> none  [shards(): lax.all_to_all(cells, 'lat', split_axis=1, concat_axis=0, tiled=True)]
    unnamed x41 -> x39, local copies, waits for them, and re-layouts: 21.5 us -> 20.2 us
  transfers between devices with their start and end apart: 9 -> 15, of which waited for: 4 -> 3; matrix products, arithmetic and copies ran while one was open for 21% -> 20% of each run, Pallas kernels for 0% -> 0%
where the time goes in v1:
time: 904 us; the launch traced here: 893 us
  local copies, waits for them, and re-layouts  332 us (37%)
  other arithmetic  216 us (24%)
  waiting for transfers between devices  178 us (20%)
  starting transfers between devices  54.6 us (6%)
  matrix products  49.2 us (5%)
  blocking collectives  49 us (5%)
  between operations  14.9 us (2%)
    scatter-add x4, other arithmetic, shards(): grad_hidden.at[:, corners[which].reshape(-1)]  182 us
    reduce_scatter x2, waiting for transfers between devices, channel_mix(): lax.psum_scatter(jnp.dot(local_weights, stacked, preferred_element_type=j...  175 us
    gather x8, local copies, waits for them, and re-layouts, shards(): jnp.take(flat_hidden, corners[which], axis=1)  141 us
    dot_general x2, local copies, waits for them, and re-layouts, channel_mix(): jnp.dot(local_weights, stacked, preferred_element_type=jnp.float32)  55.9 us
    reshape x2, local copies, waits for them, and re-layouts, tap_stack(): stacked.reshape(9 * padded_field.shape[0], row_count * padded_field.shape...  53.8 us
    dot_general x2, matrix products, channel_mix(): jnp.dot(local_weights, stacked, preferred_element_type=jnp.float32)  49.2 us
    all_to_all x1, blocking collectives, shards(): lax.all_to_all(local_departures.astype(jnp.bfloat16), 'lat', split_axis=1...  49 us
    ppermute x7, starting transfers between devices, panel_set(): lax.ppermute(current_arr, axis_key, [(q, q ^ pp) for q in range(x_next)])  37.1 us
  transfers between devices with their start and end apart: 15, of which 3 were waited for; matrix products, arithmetic and copies ran while one was open for 20% of the time, Pallas kernels for 0%

profile of v1, /device:TPU:0, one launch (start us, length us, event | category | flops | bytes accessed | tf_op | source)
XLA Modules:
  0.0 893.5 jit_solution(5450671900713569363)
XLA Ops:
  7.2 3.6 collective-permute-start.7
  10.9 1.3 collective-permute-start.8
  15.5 3.0 fusion.65
  19.6 1.8 fusion.26
  21.4 2.7 bitcast_dynamic-update-slice_fusion.5
  24.1 1.3 fusion.27
  25.4 1.9 fusion.28
  27.3 1.3 bitcast_dynamic-update-slice_fusion.4
  28.6 1.4 fusion.29
  30.0 2.9 fusion.61
  34.0 1.9 fusion.30
  35.9 2.7 bitcast_dynamic-update-slice_fusion.3
  38.6 1.3 fusion.31
  39.9 27.0 %reshape.438 = bf16[576,11520]{1,0:T(8,128)(2,1)} reshape(bf16[9,64,8,1440]{3,2,1,0:T(8,128)(2,1)} %fusion.31) | data formatting | bytes 26542080 | tf_op jit(solution)/shard_map/reshape | solution.py:71
  66.9 28.0 %dot_general.15 = bf16[8,1440,576]{1,0,2:T(8,128)(2,1)} reshape(bf16[11520,576]{0,1:T(8,128)(2,1)} %bitcast.269) | data formatting | bytes 26542080 | tf_op jit(solution)/shard_map/dot_general | solution.py:84
  94.8 24.5 %fusion.4 = bf16[256,8,1440]{2,0,1:T(8,128)(2,1)} fusion(bf16[256,576,1]{0,1,2:T(8,128)(2,1)S(1)} %bitcast.284, bf16[8,1440,576]{1,0,2:T(8,128)(2,1)} %dot_general.15), kind=kOutput, calls=%fused_computation.13 | convolution fusion | flops 3400335360 | bytes 19464192 | tf_op jit(solution)/shard_map/dot_general | solution.py:84
  120.1 4.3 collective-permute-start.6
  124.4 26.8 %collective-permute-start = (s32[1,1,1024]{2,1,0:T(1,128)S(1)}, s32[1,1,1024]{2,1,0:T(1,128)S(1)}, u32[]{:S(2)}, u32[]{:S(2)}) collective-permute-start(s32[1,1,1024]{2,1,0:T(1,128)S(1)} %get-tuple-element.66), channel_id=1, source_target_pairs={{0,4},{4,0},{8,12},{12,8},{16,20},{20,16},{24,28},{28,24},{1,5},{5... | collective-permute-start | bytes 12296 | tf_op jit(solution)/shard_map/ppermute | solution.py:31
  151.2 2.3 collective-permute-start.1
  154.7 3.8 all-to-all-start
  158.6 2.1 fusion.25
  160.7 1.8 collective-permute-start.4
  162.6 1.5 collective-permute-start.5
  164.1 3.0 collective-permute-done.5
  170.4 4.2 all-to-all-start.1
  174.7 86.1 %reduce-scatter.3.cloned.1.call-done = bf16[64,8,1440]{2,0,1:T(8,128)(2,1)} async-done(((bf16[256,8,1440]{2,0,1:T(8,128)(2,1)}), bf16[64,8,1440]{2,0,1:T(8,128)(2,1)}) %reduce-scatter.3.cloned.1.call-update) | async-done | bytes 1474576 | tf_op jit(solution)/shard_map/reduce_scatter | solution.py:83
  260.9 3.7 multiply_multiply_fusion.1
  264.5 5.6 copy.121
  270.2 30.4 %gather_fusion.3 = f32[8192,64]{1,0:T(8,128)} fusion(f32[64,11520]{0,1:T(8,128)} %bitcast.264, s32[8192]{0:T(1024)S(1)} %get-tuple-element.70), kind=kCustom, calls=%fused_computation.2.clone | custom fusion | bytes 4227072 | tf_op jit(solution)/shard_map/jit(_take)/gather | solution.py:120
  300.6 2.8 copy.100
  303.5 33.1 %gather_fusion.1 = f32[8192,64]{1,0:T(8,128)} fusion(f32[64,11520]{0,1:T(8,128)} %bitcast.265, s32[8192]{0:T(1024)} %get-tuple-element.72), kind=kCustom, calls=%fused_computation.clone | custom fusion | bytes 4227072 | tf_op jit(solution)/shard_map/jit(_take)/gather | solution.py:120
  336.6 3.8 copy.96
  340.4 33.1 %gather_fusion.2 = f32[8192,64]{1,0:T(8,128)} fusion(f32[64,11520]{0,1:T(8,128)} %bitcast.266, s32[8192]{0:T(1024)} %get-tuple-element.71), kind=kCustom, calls=%fused_computation.1.clone | custom fusion | bytes 4227072 | tf_op jit(solution)/shard_map/jit(_take)/gather | solution.py:120
  373.5 3.8 copy.98
  377.3 30.4 %gather_fusion.4 = f32[8192,64]{1,0:T(8,128)} fusion(f32[64,11520]{0,1:T(8,128)} %bitcast.267, s32[8192]{0:T(1024)S(1)} %get-tuple-element.69), kind=kCustom, calls=%fused_computation.3.clone | custom fusion | bytes 4227072 | tf_op jit(solution)/shard_map/jit(_take)/gather | solution.py:120
  407.8 3.8 copy.102
  411.6 5.7 convert_bitcast_fusion
  417.3 2.9 broadcast_multiply_fusion
  420.4 2.7 copy.105
  423.1 1.7 copy.129
  424.9 2.8 copy.107
  427.6 1.7 copy.130
  429.4 2.8 copy.109
  432.2 1.7 copy.131
  433.9 2.8 copy.111
  436.7 47.2 %scatter_custom_fusion = f32[64,11520]{0,1:T(8,128)} fusion(s32[8192]{0:T(1024)} %bitcast.290, f32[8192,64]{1,0:T(8,128)} %copy.105, f32[]{:T(128)} %constant.40.clone.1), kind=kCustom, calls=%fused_computation.25 | custom fusion | flops 524288 | bytes 2949632 | tf_op jit(solution)/shard_map/scatter-add | solution.py:127
  483.9 45.1 %scatter_fusion = f32[64,11520]{0,1:T(8,128)} fusion(f32[64,11520]{0,1:T(8,128)} %scatter_custom_fusion, s32[8192]{0:T(1024)S(1)} %bitcast.288, f32[8192,64]{1,0:T(8,128)} %copy.107), kind=kCustom, calls=%fused_computation.6 | custom fusion | flops 524288 | bytes 6324224 | tf_op jit(solution)/shard_map/scatter-add | solution.py:127
  528.9 45.2 %scatter_fusion.1 = f32[64,11520]{0,1:T(8,128)} fusion(f32[64,11520]{0,1:T(8,128)} %scatter_fusion, s32[8192]{0:T(1024)S(1)} %bitcast.287, f32[8192,64]{1,0:T(8,128)} %copy.109), kind=kCustom, calls=%fused_computation.7 | custom fusion | flops 524288 | bytes 6324224 | tf_op jit(solution)/shard_map/scatter-add | solution.py:127
  574.1 45.1 %scatter_fusion.2 = f32[64,11520]{0,1:T(8,128)} fusion(f32[64,11520]{0,1:T(8,128)} %scatter_fusion.1, s32[8192]{0:T(1024)S(1)} %bitcast.286, f32[8192,64]{1,0:T(8,128)} %copy.111), kind=kCustom, calls=%fused_computation.8 | custom fusion | flops 524288 | bytes 6324224 | tf_op jit(solution)/shard_map/scatter-add | solution.py:127
  619.2 6.2 copy.113
  625.3 3.1 fusion.15
  628.4 1.3 collective-permute-start.9
  629.7 3.1 collective-permute-start.10
  633.0 1.2 fusion.58
  634.2 1.2 fusion.60
  640.0 21.6 %copy.114 = bf16[9,64,8,1440]{3,2,1,0:T(8,128)(2,1)} copy(bf16[9,64,8,1440]{3,1,2,0:T(8,128)(2,1)S(1)} %fusion.37) | data formatting | bytes 26542080 | tf_op jit(solution)/shard_map/stack | solution.py:70
  661.7 26.8 %reshape.445 = bf16[576,11520]{1,0:T(8,128)(2,1)} reshape(bf16[9,64,8,1440]{3,2,1,0:T(8,128)(2,1)} %copy.114) | data formatting | bytes 26542080 | tf_op jit(solution)/shard_map/reshape | solution.py:71
  688.4 27.9 %dot_general.18 = bf16[8,1440,576]{1,0,2:T(8,128)(2,1)} reshape(bf16[11520,576]{0,1:T(8,128)(2,1)} %bitcast.270) | data formatting | bytes 26542080 | tf_op jit(solution)/shard_map/dot_general | solution.py:84
  716.4 24.7 %fusion.7 = bf16[256,8,1440]{2,0,1:T(8,128)(2,1)} fusion(bf16[256,576,1]{0,1,2:T(8,128)(2,1)S(1)} %bitcast.285, bf16[8,1440,576]{1,0,2:T(8,128)(2,1)} %dot_general.18), kind=kOutput, calls=%fused_computation.14 | convolution fusion | flops 3400335360 | bytes 19464192 | tf_op jit(solution)/shard_map/dot_general | solution.py:84
  741.1 1.2 copy-done.3
  742.3 49.0 %all_to_all.12 = bf16[64,8,1,1024]{3,0,2,1:T(8,128)(2,1)S(1)} all-to-all(bf16[64,8,1,1024]{3,0,2,1:T(8,128)(2,1)S(1)} %copy-done.3), channel_id=1, replica_groups=mesh['lat'=8,'chan'=4] {'lat'}, dimensions={1} | all-to-all | bytes 2097152 | tf_op jit(solution)/shard_map/all_to_all | solution.py:122
  791.6 2.5 copy.118
  794.2 88.7 %reduce-scatter.5.cloned.1.call-done = bf16[64,8,1440]{2,0,1:T(8,128)(2,1)} async-done(((bf16[256,8,1440]{2,0,1:T(8,128)(2,1)}), bf16[64,8,1440]{2,0,1:T(8,128)(2,1)}) %reduce-scatter.5.cloned.1.call-update) | async-done | bytes 1474576 | tf_op jit(solution)/shard_map/reduce_scatter | solution.py:83
  882.9 3.4 copy.117
  (82 shorter events, 15.9 us)
Async XLA Ops:
  7.2 5.0 copy-start
  7.2 7.3 copy-start.1
  7.2 253.7 %reduce-scatter.3.cloned.1.call-start = ((), (), s32[]{:S(2)}) async-start(), calls=%async_computation.5 | async-start | bytes 7864320 | tf_op jit(solution)/shard_map/reduce_scatter | solution.py:83
  7.2 8.3 collective-permute-start.7
  10.9 19.1 %collective-permute-start.8 = (bf16[64,8,1440]{2,1,0:T(8,128)(2,1)}, bf16[64,8,1440]{2,1,0:T(8,128)(2,1)}, u32[]{:S(2)}, u32[]{:S(2)}) collective-permute-start(bf16[64,8,1440]{2,1,0:T(8,128)(2,1)} %param.9), channel_id=1, source_target_pairs={{4,0},{8,4},{12,8},{16,12},{20,16},{24,20},{28,24},{5,1},{9,5},{13... | collective-permute-start | bytes 4423688 | tf_op jit(solution)/shard_map/ppermute | solution.py:45
  66.9 28.0 %copy-start.5 = (bf16[256,3,3,64]{0,3,2,1:T(8,128)(2,1)S(1)}, bf16[256,3,3,64]{0,3,2,1:T(8,128)(2,1)}, u32[]{:S(2)}) copy-start(bf16[256,3,3,64]{0,3,2,1:T(8,128)(2,1)} %copy.92) | copy-start | bytes 884740
  119.4 0.8 copy-start.9
  119.4 34.6 %copy-start.12 = (s32[1,8]{1,0:T(1,128)S(1)}, s32[1,8]{1,0:T(1,128)}, u32[]{:S(2)}) copy-start(s32[1,8]{1,0:T(1,128)} %param.15) | copy-start | bytes 100
  119.4 34.7 %copy-start.6 = (bf16[4,1,8,1024]{3,2,1,0:T(8,128)(2,1)S(1)}, bf16[4,1,8,1024]{3,2,1,0:T(8,128)(2,1)}, u32[]{:S(2)}) copy-start(bf16[4,1,8,1024]{3,2,1,0:T(8,128)(2,1)} %param.13) | copy-start | bytes 196612
  119.4 39.2 %copy-start.4 = (f32[64,1,8,1024]{3,2,1,0:T(8,128)S(1)}, f32[64,1,8,1024]{3,2,1,0:T(8,128)}, u32[]{:S(2)}) copy-start(f32[64,1,8,1024]{3,2,1,0:T(8,128)} %param.12) | copy-start | bytes 6291460
  120.1 40.6 %collective-permute-start.6 = (s32[1,1,1024]{2,1,0:T(1,128)S(1)}, s32[1,1,1024]{2,1,0:T(1,128)S(1)}, u32[]{:S(2)}, u32[]{:S(2)}) collective-permute-start(s32[1,1,1024]{2,1,0:T(1,128)S(1)} %get-tuple-element.61), channel_id=1, source_target_pairs={{0,28},{4,24},{8,20},{12,16},{16,12},{20,8},{24,4},{28,0},{1,29},{... | collective-permute-start | bytes 12296 | tf_op jit(solution)/shard_map/ppermute | solution.py:31
  124.4 38.1 %collective-permute-start = (s32[1,1,1024]{2,1,0:T(1,128)S(1)}, s32[1,1,1024]{2,1,0:T(1,128)S(1)}, u32[]{:S(2)}, u32[]{:S(2)}) collective-permute-start(s32[1,1,1024]{2,1,0:T(1,128)S(1)} %get-tuple-element.66), channel_id=1, source_target_pairs={{0,4},{4,0},{8,12},{12,8},{16,20},{20,16},{24,28},{28,24},{1,5},{5... | collective-permute-start | bytes 12296 | tf_op jit(solution)/shard_map/ppermute | solution.py:31
  151.2 12.8 %collective-permute-start.1 = (s32[1,1,1024]{2,1,0:T(1,128)S(1)}, s32[1,1,1024]{2,1,0:T(1,128)S(1)}, u32[]{:S(2)}, u32[]{:S(2)}) collective-permute-start(s32[1,1,1024]{2,1,0:T(1,128)S(1)} %get-tuple-element.65), channel_id=1, source_target_pairs={{0,8},{4,12},{8,0},{12,4},{16,24},{20,28},{24,16},{28,20},{1,9},{5... | collective-permute-start | bytes 12296 | tf_op jit(solution)/shard_map/ppermute | solution.py:31
  153.6 10.5 %collective-permute-start.2 = (s32[1,1,1024]{2,1,0:T(1,128)S(1)}, s32[1,1,1024]{2,1,0:T(1,128)S(1)}, u32[]{:S(2)}, u32[]{:S(2)}) collective-permute-start(s32[1,1,1024]{2,1,0:T(1,128)S(1)} %get-tuple-element.64), channel_id=1, source_target_pairs={{0,12},{4,8},{8,4},{12,0},{16,28},{20,24},{24,20},{28,16},{1,13},{... | collective-permute-start | bytes 12296 | tf_op jit(solution)/shard_map/ppermute | solution.py:31
  153.6 10.5 %collective-permute-start.3 = (s32[1,1,1024]{2,1,0:T(1,128)S(1)}, s32[1,1,1024]{2,1,0:T(1,128)S(1)}, u32[]{:S(2)}, u32[]{:S(2)}) collective-permute-start(s32[1,1,1024]{2,1,0:T(1,128)S(1)} %get-tuple-element.63), channel_id=1, source_target_pairs={{0,16},{4,20},{8,24},{12,28},{16,0},{20,4},{24,8},{28,12},{1,17},{... | collective-permute-start | bytes 12296 | tf_op jit(solution)/shard_map/ppermute | solution.py:31
  154.7 15.7 %all-to-all-start = ((bf16[4,1,8,1024]{3,0,1,2:T(4,128)(2,1)}), bf16[4,1,8,1024]{3,0,1,2:T(4,128)(2,1)S(1)}, u32[]{:S(2)}, u32[]{:S(2)}) async-start(bf16[4,1,8,1024]{3,0,1,2:T(4,128)(2,1)} %multiply_convert_fusion), calls=%async_computation | async-start | bytes 131072 | tf_op jit(solution)/shard_map/all_to_all | solution.py:108
  160.7 100.2 %copy-start.10 = (f32[64]{0:T(128)S(1)}, f32[64]{0:T(128)}, u32[]{:S(2)}) copy-start(f32[64]{0:T(128)} %param.11) | copy-start | bytes 772
  160.7 3.4 collective-permute-start.4
  162.6 4.5 collective-permute-start.5
  170.4 241.2 %all-to-all-start.1 = ((bf16[64,1,8,1024]{3,0,1,2:T(8,128)(2,1)}), bf16[64,1,8,1024]{3,0,1,2:T(8,128)(2,1)}, u32[]{:S(2)}, u32[]{:S(2)}) async-start(bf16[64,1,8,1024]{3,0,1,2:T(8,128)(2,1)} %fusion.25), calls=%async_computation.2 | async-start | bytes 2097152 | tf_op jit(solution)/shard_map/all_to_all | solution.py:105
  174.6 708.2 %reduce-scatter.5.cloned.1.call-start = ((), (), s32[]{:S(2)}) async-start(), calls=%async_computation.6 | async-start | bytes 7864320 | tf_op jit(solution)/shard_map/reduce_scatter | solution.py:83
  407.8 3.8 copy-start.7
  407.8 3.8 copy-start.8
  619.2 6.2 copy-start.2
  619.2 6.2 copy-start.11
  628.4 5.8 collective-permute-start.9
  629.7 7.9 collective-permute-start.10
  741.1 1.2 copy-start.3
Sparse Core Ops, SparseCore 0:
  119.5 141.3 reduce-scatter.2
  741.2 141.5 reduce-scatter.4
